TPU v7x, 128 devices: a whole 4x4x4 slice. The times are simulated.
128 devices in a mesh: fx: 16 (over x, z), fy: 8 (over y, core).
Axes of the slice: x: 4, y: 4, z: 4, core: 2. Of those that a mesh axis runs over, the one named last changes fastest.
Arguments:
- fluid_state: float32 [5, 8, 2048, 1024], P(None, None, 'fx', 'fy'), may hold values from -0.3 to 2.8, as said below
- surface_points: float32 [16384, 3, 128], P(('fx', 'fy')), may hold values from 0 to 1
- surface_normals: float32 [16384, 3, 128], P(('fx', 'fy')), may hold values from -1 to 1
- owner_ids: int32 [16384, 1], P(('fx', 'fy')), may hold values from 0 to 127; in each aligned block of 128 rows (0 to 127, 128 to 255, ...) at most 2 rows name the same one
- support_ids: int32 [16384, 2], P(('fx', 'fy')), may hold values from 0 to 7
- struct_points: float32 [1024, 3, 128], P(('fx', 'fy')), may hold values from 0 to 1
- couplings: float32 [1024, 4, 128, 128], P(('fx', 'fy')), may hold values from 0.5 to 1
- coupling_pattern: int32 [1024, 4], P(('fx', 'fy')), may hold values from 0 to 7, as said below
- stiff_diagonal: float32 [1024, 128], P(('fx', 'fy')), may hold values from 1.05 to 1.6
- struct_load: float32 [1024, 3, 128], P(('fx', 'fy')), may hold values from -6 to 6
- predicted: float32 [1024, 3, 128], P(('fx', 'fy')), may hold values from -3 to 3
- hist_residual: float32 [8, 1024, 3, 128], P(None, ('fx', 'fy')), may hold values from -0.03 to 0.03
- hist_response: float32 [8, 1024, 3, 128], P(None, ('fx', 'fy')), may hold values from -6 to 6
Outputs:
- new_state: float32 [5, 8, 2048, 1024], P(None, None, 'fx', 'fy')
- next_estimate: float32 [1024, 3, 128], P(('fx', 'fy'))
- coupling_residual: float32 [1024, 3, 128], P(('fx', 'fy'))
Inputs may be any that keep to these rules, and one draw needn't show every extreme that they name: `fluid_state`: component 0 (density) lies in [0.8, 1.2], components 1 to 3 (momenta) in [-0.3, 0.3], component 4 (total energy) in [2.2, 2.8]. `owner_ids`: among the 128 surface blocks of one device (aligned blocks of rows), no owner is named by more than 2 of them. `support_ids`: local block numbers on the owner. For each device's 8 structure blocks and each column k, the entries coupling_pattern[., k] are a permutation of 0 to 7.
All inputs are finite; a program needn't handle non-finite values.
Results may differ from a plain program's by a relative error of at most 0.0003.
Values sent between devices are 32-bit elements; how exact they have to be, the bound alone decides.
No kernel may reach another device: no remote copies, remote signals or barrier semaphores. Data moves between devices by JAX's collectives and lax.ppermute only.
A program may use at most 192 MiB of HBM per device.

v0:
```python
import math
import jax
import jax.numpy as jnp
from jax import lax
from jax.sharding import PartitionSpec as P

CG_ITERS = 2
COUPLE = 2
TOP_PRECISION = lax.Precision.HIGHEST
STEP_RATIO = 0.12
WALL_SPEED = 0.5
WALL_GAIN = 0.5
LOAD_SCALE = 4.0
PRESSURE_REF = 0.98
RADIUS = 1.0


def with_halo(cells, sides, width):
    for axis, dim in sides:
        count = lax.axis_size(axis)
        head = lax.slice_in_dim(cells, 0, width, axis=dim)
        tail = lax.slice_in_dim(cells, cells.shape[dim] - width, cells.shape[dim], axis=dim)
        cells = jnp.concatenate(
            [
                lax.ppermute(tail, axis, [(i, (i + 1) % count) for i in range(count)]),
                cells,
                lax.ppermute(head, axis, [((i + 1) % count, i) for i in range(count)]),
            ],
            axis=dim,
        )
    return cells


def state_pressure(state):
    return 0.4 * (
        state[4]
        - 0.5 * (state[1] * state[1] + state[2] * state[2] + state[3] * state[3]) / state[0]
    )


def face_terms(state, momentum):
    density = state[0]
    velocity = state[momentum] / density
    pressure = state_pressure(state)
    flux = state * velocity
    flux = flux.at[momentum].add(pressure)
    flux = flux.at[4].add(pressure * velocity)
    speed = jnp.abs(velocity) + jnp.sqrt(1.4 * pressure / density)
    return (flux, speed)


def rusanov(left, right, left_flux, right_flux, left_speed, right_speed):
    return 0.5 * (left_flux + right_flux) - 0.5 * jnp.maximum(left_speed, right_speed) * (
        right - left
    )


def vertical_terms(state, wall):
    bottom = state[:, 0]
    ghost = bottom.at[3].set(2.0 * bottom[0] * wall - bottom[3])
    column = jnp.concatenate([ghost[:, None], state, state[:, -1:]], axis=1)
    flux, speed = face_terms(column, 3)
    faces = rusanov(column[:, :-1], column[:, 1:], flux[:, :-1], flux[:, 1:], speed[:-1], speed[1:])
    return faces[:, 1:] - faces[:, :-1]


def horizontal_terms(state):
    extended = with_halo(state, (("fx", 2), ("fy", 3)), 1)
    strip = extended[:, :, :, 1:-1]
    flux, speed = face_terms(strip, 1)
    faces = rusanov(
        strip[:, :, :-1],
        strip[:, :, 1:],
        flux[:, :, :-1],
        flux[:, :, 1:],
        speed[:, :-1],
        speed[:, 1:],
    )
    total = faces[:, :, 1:] - faces[:, :, :-1]
    strip = extended[:, :, 1:-1, :]
    flux, speed = face_terms(strip, 2)
    faces = rusanov(
        strip[:, :, :, :-1],
        strip[:, :, :, 1:],
        flux[:, :, :, :-1],
        flux[:, :, :, 1:],
        speed[:, :, :-1],
        speed[:, :, 1:],
    )
    return total + (faces[:, :, :, 1:] - faces[:, :, :, :-1])


def kernel_block(fluid_points, struct_nodes):
    squared = jnp.zeros((), jnp.float32)
    for axis in range(3):
        offset = fluid_points[..., axis, :, None] - struct_nodes[..., axis, None, :]
        squared = squared + offset * offset
    ratio = jnp.sqrt(squared) / RADIUS
    reach = jnp.maximum(1.0 - ratio, 0.0)
    return reach * reach * reach * reach * (4.0 * ratio + 1.0)


def owner_kernels(places, support, struct_points):
    rows = places.shape[0]
    points = places.shape[-1]
    spread = support.shape[1]
    group = math.gcd(rows, 16)

    def one_group(inputs):
        where, which = inputs
        return kernel_block(where[:, None], struct_points[which])

    kernels = lax.map(
        one_group, (places.reshape(-1, group, 3, points), support.reshape(-1, group, spread))
    )
    return kernels.reshape(rows, spread, points, points)


def owner_motion(kernels, support, field_values):
    return jnp.einsum("gkij,gkcj->gci", kernels, field_values[support], precision=TOP_PRECISION)


def owner_loads(kernels, support, blocks, traction):
    flux_terms = jnp.einsum("gkij,gci->gkcj", kernels, traction, precision=TOP_PRECISION)
    selector = (support[:, :, None] == jnp.arange(blocks, dtype=jnp.int32)[None, None, :]).astype(
        jnp.float32
    )
    return jnp.einsum("rke,rkcj->ecj", selector, flux_terms, precision=TOP_PRECISION)


def route_coords(geometry, support):
    moved_geometry, moved_support = (
        lax.all_to_all(geometry, ("fx", "fy"), split_axis=0, concat_axis=0, tiled=True),
        lax.all_to_all(support, ("fx", "fy"), split_axis=0, concat_axis=0, tiled=True),
    )
    return (moved_geometry, moved_support)


def route_field(values):
    return lax.all_to_all(values, ("fx", "fy"), split_axis=0, concat_axis=0, tiled=True)


def global_sums(values):
    return lax.psum(values, ("fx", "fy"))


def stiffness(field_values, couplings, sparsity_layout, selector, diagonal):
    blocks = field_values.shape[0]
    scale = 1.0 / (2.0 * couplings.shape[1] * couplings.shape[2])
    flux_terms = jnp.einsum("aosq,avs->aovq", couplings, field_values, precision=TOP_PRECISION)
    shipped = jnp.einsum("bke,bkdj->edj", selector, flux_terms, precision=TOP_PRECISION)
    stacked = jnp.concatenate([shipped, field_values], axis=0)
    extended = with_halo(stacked, ((("fx", "fy"), 0),), blocks)
    prior_iterate = extended[:blocks]
    later = extended[-blocks:]
    forward_pass = jnp.einsum(
        "hzwm,hzlm->hlw", couplings, prior_iterate[sparsity_layout], precision=TOP_PRECISION
    )
    return diagonal[:, None, :] * field_values - scale * (forward_pass + later)


def conjugate(start, rhs, operate):
    residual = rhs - operate(start)
    solution = start
    direction = residual
    norm_now = global_sums(jnp.stack([jnp.sum(residual * residual)]))[0]
    for count in range(CG_ITERS):
        image = operate(direction)
        alpha = norm_now / global_sums(jnp.stack([jnp.sum(direction * image)]))[0]
        solution = solution + alpha * direction
        residual = residual - alpha * image
        if count + 1 < CG_ITERS:
            norm_next = global_sums(jnp.stack([jnp.sum(residual * residual)]))[0]
            direction = residual + norm_next / norm_now * direction
            norm_now = norm_next
    return solution


def newton_update(response, gram, projected, responses):
    lower = jnp.linalg.cholesky(gram)
    middle = lax.linalg.triangular_solve(lower, projected[:, None], left_side=True, lower=True)
    weights = lax.linalg.triangular_solve(
        lower, middle, left_side=True, lower=True, transpose_a=True
    )[:, 0]
    return response - jnp.einsum("h,hbdp->bdp", weights, responses, precision=TOP_PRECISION)


def on_device(
    fluid_state,
    surface_points,
    surface_normals,
    owner_ids,
    support_ids,
    struct_points,
    couplings,
    coupling_pattern,
    stiff_diagonal,
    struct_load,
    predicted,
    hist_residual,
    hist_response,
):
    rows_fx = lax.axis_size("fx")
    rows_fy = lax.axis_size("fy")
    devices = rows_fx * rows_fy
    surface_count = owner_ids.shape[0]
    capacity = max(2, 2 * surface_count // devices)
    owners = owner_ids[:, 0]
    chosen = (owners[:, None] == jnp.arange(devices, dtype=jnp.int32)[None, :]).astype(jnp.int32)
    slots = owners * capacity + jnp.sum((jnp.cumsum(chosen, axis=0) - chosen) * chosen, axis=1)
    width = devices * capacity

    def pack(values):
        return jnp.zeros((width,) + values.shape[1:], values.dtype).at[slots].set(values)

    owner_geometry, owner_support = route_coords(pack(surface_points), pack(support_ids))
    kernels = owner_kernels(owner_geometry, owner_support, struct_points)
    blocks = couplings.shape[0]
    selector = (
        coupling_pattern[:, :, None] == jnp.arange(blocks, dtype=jnp.int32)[None, None, :]
    ).astype(jnp.float32)

    def operate(field_values):
        return stiffness(field_values, couplings, coupling_pattern, selector, stiff_diagonal)

    horizontal = horizontal_terms(fluid_state)
    estimate = predicted
    differences = hist_residual
    responses = hist_response
    last_residual = predicted
    last_response = predicted
    new_state = fluid_state
    residual = predicted
    for count in range(COUPLE):
        motion_slots = owner_motion(kernels, owner_support, estimate)
        motion = route_field(motion_slots)[slots]
        wall = WALL_SPEED * jnp.tanh(WALL_GAIN * jnp.sum(surface_normals * motion, axis=1))
        new_state = fluid_state - STEP_RATIO * (horizontal + vertical_terms(fluid_state, wall))
        pressure = state_pressure(new_state[:, 0])
        traction = -LOAD_SCALE * (pressure - PRESSURE_REF)[:, None, :] * surface_normals
        owner_traction = route_field(pack(traction))
        loads = owner_loads(kernels, owner_support, blocks, owner_traction)
        response = conjugate(estimate, struct_load + loads, operate)
        residual = response - estimate
        if count > 0:
            differences = jnp.concatenate(
                [differences[1:], (residual - last_residual)[None]], axis=0
            )
            responses = jnp.concatenate([responses[1:], (response - last_response)[None]], axis=0)
        last_residual = residual
        last_response = response
        gram = jnp.einsum("hbdp,gbdp->hg", differences, differences, precision=TOP_PRECISION)
        projected = jnp.einsum("hbdp,bdp->h", differences, residual, precision=TOP_PRECISION)
        totals = global_sums(jnp.concatenate([gram, projected[:, None]], axis=1))
        estimate = newton_update(response, totals[:, :-1], totals[:, -1], responses)
    return (new_state, estimate, residual)


def solution(mesh):
    placed = (
        P(None, None, "fx", "fy"),
        P(("fx", "fy"), None, None),
        P(("fx", "fy"), None, None),
        P(("fx", "fy"), None),
        P(("fx", "fy"), None),
        P(("fx", "fy"), None, None),
        P(("fx", "fy"), None, None, None),
        P(("fx", "fy"), None),
        P(("fx", "fy"), None),
        P(("fx", "fy"), None, None),
        P(("fx", "fy"), None, None),
        P(None, ("fx", "fy"), None, None),
        P(None, ("fx", "fy"), None, None),
    )
    return jax.shard_map(
        on_device,
        mesh=mesh,
        in_specs=placed,
        out_specs=(
            P(None, None, "fx", "fy"),
            P(("fx", "fy"), None, None),
            P(("fx", "fy"), None, None),
        ),
        check_vma=False,
    )
```

profile of v0, /device:TPU:1, one launch (start us, length us, event | category | flops | bytes accessed | tf_op | source)
XLA Modules:
  0.0 1005.2 jit_solution(8151141601063758827)
XLA Ops:
  6.5 11.5 %all-to-all-start = ((s32[128,2,2]{1,2,0:T(2,128)}), s32[128,2,2]{1,2,0:T(2,128)S(1)}, u32[]{:S(2)}, u32[]{:S(2)}) async-start(s32[128,2,2]{1,2,0:T(2,128)} %copy.261), calls=%async_computation | async-start | bytes 262144 | tf_op jit(solution)/shard_map/all_to_all | solution.py:134
  19.6 5.4 collective-permute-start.1
  32.7 12.5 %scatter_fusion = f32[256,3,128]{2,1,0:T(4,128)} fusion(f32[256,3,128]{2,1,0:T(4,128)} %broadcast.438.clone, s32[128]{0:T(128)S(1)} %fusion.166, f32[128,3,128]{2,1,0:T(4,128)S(1)} %copy.265), kind=kCustom, calls=%fused_computation.12 | custom fusion | bytes 590336 | tf_op jit(solution)/shard_map/scatter | solution.py:214
  45.2 15.0 %all-to-all-start.1 = ((f32[256,3,128]{2,1,0:T(4,128)}), f32[256,3,128]{2,1,0:T(4,128)}, u32[]{:S(2)}, u32[]{:S(2)}) async-start(f32[256,3,128]{2,1,0:T(4,128)} %scatter_fusion), calls=%async_computation.1 | async-start | bytes 1048576 | tf_op jit(solution)/shard_map/all_to_all | solution.py:133
  65.0 3.3 fusion.182
  70.4 3.3 copy.253
  75.3 3.9 copy.254
  87.1 3.2 copy.255
  90.4 3.2 copy.256
  93.6 5.9 pad_maximum_fusion
  100.7 3.1 slice_multiply_fusion
  103.8 3.0 fusion.26
  112.6 69.3 %while.20 = (s32[]{:T(128)}, f32[16,16,2,128,128]{4,3,2,1,0:T(8,128)}, f32[16,16,3,128]{3,1,2,0:T(8,128)}, s32[16,16,2]{1,0,2:T(8,128)S(1)}, f32[8,3,128]{2,1,0:T(4,128)S(1)}, /*index=5*/s32[]{:T(128)}) while((s32[]{:T(128)}, f32[16,16,2,128,128]{4,3,2,1,0:T(8,128)}, f32[16,16,3,128]{3,1,2,0:T(8,128)}, s32[16,16,2]{1,0,2:T(8,128)S(1)}, ...), condition=%wide.region_5.6_spmd, body=%wide.region_4.5_spmd.sunk | while | flops 8389730 | bytes 2471257 | solution.py:113
  114.2 2.8 fusion.215
  118.6 2.7 fusion.215
  122.9 2.7 fusion.215
  127.3 2.7 fusion.215
  135.9 2.7 fusion.215
  140.3 2.7 fusion.215
  144.6 2.7 fusion.215
  148.9 2.8 fusion.215
  153.3 2.7 fusion.215
  157.6 2.7 fusion.215
  161.9 2.7 fusion.215
  170.6 2.7 fusion.215
  179.2 2.7 fusion.215
  182.0 32.0 %convolution_bitcast_fusion.3 = f32[256,3,128]{2,1,0:T(4,128)} fusion(f32[256,2,128,128]{3,2,1,0:T(8,128)} %bitcast.465, f32[256,2,3,128]{3,1,0,2:T(2,128)S(1)} %bitcast.471), kind=kOutput, calls=%fused_computation.76 | convolution fusion | flops 301989888 | bytes 34734080 | tf_op jit(solution)/shard_map/gkij,gkcj->gci/dot_general | solution.py:120
  213.9 10.2 %all-to-all-start.2 = ((f32[256,3,128]{2,1,0:T(4,128)}), f32[256,3,128]{2,1,0:T(4,128)}, u32[]{:S(2)}, u32[]{:S(2)}) async-start(f32[256,3,128]{2,1,0:T(4,128)} %convolution_bitcast_fusion.3), calls=%async_computation.2 | async-start | bytes 1048576 | tf_op jit(solution)/shard_map/all_to_all | solution.py:140
  224.2 11.7 %fusion.4 = f32[5,8,128,129]{3,2,1,0:T(8,128)} fusion(f32[5,8,130,1]{3,2,1,0:T(8,128)} %copy.255, f32[5,8,1,128]{3,2,1,0:T(1,128)S(1)} %bitcast.482, f32[5,8,128,128]{3,2,1,0:T(8,128)} %param.40, f32[5,8,1,128]{3,2,1,0:T(1,128)S(1)} %bitcast.487, f32[5,8,130,1]{3,2,1,0:T(8,128)} %copy.256, f32[5,8,128,130]{3,2,1,0:T(8,128)} %fusion.25, f32[8,128,129]{2,1,0:T(8,128)} %fusion.24), kind=kLoop, calls=%fused_computation.29 | loop fusion | flops 7265280 | bytes 11158144 | tf_op jit(solution)/shard_map/sub | solution.py:53
  252.1 12.4 %scatter_fusion.1 = f32[256,3,128]{2,1,0:T(4,128)} fusion(f32[256,3,128]{2,1,0:T(4,128)} %broadcast.438.clone.1, s32[128]{0:T(128)S(1)} %fusion.166, f32[128,3,128]{2,1,0:T(4,128)S(1)} %copy.273), kind=kCustom, calls=%fused_computation.13 | custom fusion | bytes 590336 | tf_op jit(solution)/shard_map/scatter | solution.py:214
  264.5 9.2 all-to-all-start.3
  276.7 10.5 %all-to-all-done.3 = f32[256,3,128]{2,1,0:T(4,128)S(1)} async-done(((f32[256,3,128]{2,1,0:T(4,128)}), f32[256,3,128]{2,1,0:T(4,128)S(1)}, u32[]{:S(2)}, u32[]{:S(2)}) %all-to-all-start.3) | async-done | bytes 393248 | tf_op jit(solution)/shard_map/all_to_all | solution.py:140
  287.2 19.6 %convolution_bitcast_fusion.1 = f32[256,2,3,128]{3,2,1,0:T(4,128)S(1)} fusion(f32[256,2,128,128]{3,2,1,0:T(8,128)} %bitcast.466, f32[256,3,128]{2,1,0:T(4,128)S(1)} %all-to-all-done.3), kind=kOutput, calls=%fused_computation.74 | convolution fusion | flops 301989888 | bytes 34734080 | tf_op jit(solution)/shard_map/gkij,gci->gkcj/dot_general | solution.py:124
  314.2 71.7 %all-reduce.1 = (f32[1]{0:T(128)}, f32[1]{0:T(128)}) all-reduce(f32[1]{0:T(128)} %bitcast.55, f32[1]{0:T(128)} %bitcast.63), channel_id=1, replica_groups=mesh['fx'=16,'fy'=8] {'fx','fy'}, use_global_device_ids=true, to_apply=%region_9.10 | all-reduce | flops 2 | bytes 16 | tf_op jit(solution)/shard_map/psum | solution.py:144
  388.0 62.7 %psum.72 = f32[1]{0:T(128)} all-reduce(f32[1]{0:T(128)} %bitcast.65), channel_id=1, replica_groups=mesh['fx'=16,'fy'=8] {'fx','fy'}, use_global_device_ids=true, to_apply=%region_13.14 | all-reduce | flops 1 | bytes 8 | tf_op jit(solution)/shard_map/psum | solution.py:144
  459.2 70.4 %psum.73 = f32[1]{0:T(128)} all-reduce(f32[1]{0:T(128)} %bitcast.74), channel_id=1, replica_groups=mesh['fx'=16,'fy'=8] {'fx','fy'}, use_global_device_ids=true, to_apply=%region_15.16 | all-reduce | flops 1 | bytes 8 | tf_op jit(solution)/shard_map/psum | solution.py:144
  531.3 62.6 %psum.74 = f32[8,9]{0,1:T(8,128)S(1)} all-reduce(f32[8,9]{0,1:T(8,128)S(1)} %pad_maximum_fusion.17), channel_id=1, replica_groups=mesh['fx'=16,'fy'=8] {'fx','fy'}, use_global_device_ids=true, to_apply=%region_16.17 | all-reduce | flops 72 | bytes 576 | tf_op jit(solution)/shard_map/psum | solution.py:144
  599.2 31.6 %convolution_bitcast_fusion.2 = f32[256,3,128]{2,1,0:T(4,128)} fusion(f32[256,2,3,128]{3,2,1,0:T(4,128)S(1)} %bitcast.472, f32[256,2,128,128]{3,2,1,0:T(8,128)} %bitcast.467), kind=kOutput, calls=%fused_computation.75 | convolution fusion | flops 301989888 | bytes 34734080 | tf_op jit(solution)/shard_map/gkij,gkcj->gci/dot_general | solution.py:120
  630.9 5.4 all-to-all-start.4
  639.1 10.9 %all-to-all-done.4 = f32[256,3,128]{2,1,0:T(4,128)S(1)} async-done(((f32[256,3,128]{2,1,0:T(4,128)}), f32[256,3,128]{2,1,0:T(4,128)S(1)}, u32[]{:S(2)}, u32[]{:S(2)}) %all-to-all-start.4) | async-done | bytes 393248 | tf_op jit(solution)/shard_map/all_to_all | solution.py:140
  664.4 12.4 %scatter_fusion.2 = f32[256,3,128]{2,1,0:T(4,128)} fusion(f32[256,3,128]{2,1,0:T(4,128)} %broadcast.438, s32[128]{0:T(128)S(1)} %copy-done.27, f32[128,3,128]{2,1,0:T(4,128)S(1)} %copy.296), kind=kCustom, calls=%fused_computation.14 | custom fusion | bytes 590336 | tf_op jit(solution)/shard_map/scatter | solution.py:214
  676.8 4.6 all-to-all-start.5
  686.7 8.3 all-to-all-done.5
  695.0 19.6 %convolution_bitcast_fusion = f32[256,2,3,128]{3,2,1,0:T(4,128)S(1)} fusion(f32[256,2,128,128]{3,2,1,0:T(8,128)} %bitcast.468, f32[256,3,128]{2,1,0:T(4,128)S(1)} %all-to-all-done.5), kind=kOutput, calls=%fused_computation.73 | convolution fusion | flops 301989888 | bytes 34734080 | tf_op jit(solution)/shard_map/gkij,gci->gkcj/dot_general | solution.py:124
  721.3 71.7 %all-reduce = (f32[1]{0:T(128)}, f32[1]{0:T(128)}) all-reduce(f32[1]{0:T(128)} %bitcast.119, f32[1]{0:T(128)} %bitcast.127), channel_id=1, replica_groups=mesh['fx'=16,'fy'=8] {'fx','fy'}, use_global_device_ids=true, to_apply=%region_22.26 | all-reduce | flops 2 | bytes 16 | tf_op jit(solution)/shard_map/psum | solution.py:144
  795.0 62.5 %psum.77 = f32[1]{0:T(128)} all-reduce(f32[1]{0:T(128)} %bitcast.129), channel_id=1, replica_groups=mesh['fx'=16,'fy'=8] {'fx','fy'}, use_global_device_ids=true, to_apply=%region_26.30 | all-reduce | flops 1 | bytes 8 | tf_op jit(solution)/shard_map/psum | solution.py:144
  866.1 70.4 %psum.78 = f32[1]{0:T(128)} all-reduce(f32[1]{0:T(128)} %bitcast.138), channel_id=1, replica_groups=mesh['fx'=16,'fy'=8] {'fx','fy'}, use_global_device_ids=true, to_apply=%region_28.32 | all-reduce | flops 1 | bytes 8 | tf_op jit(solution)/shard_map/psum | solution.py:144
  938.5 62.6 %psum.79 = f32[8,9]{0,1:T(8,128)S(1)} all-reduce(f32[8,9]{0,1:T(8,128)S(1)} %pad_maximum_fusion.18), channel_id=1, replica_groups=mesh['fx'=16,'fy'=8] {'fx','fy'}, use_global_device_ids=true, to_apply=%region_29.33 | all-reduce | flops 72 | bytes 576 | tf_op jit(solution)/shard_map/psum | solution.py:144
  (398 shorter events, 153.0 us)
Async XLA Ops:
  0.6 24.4 %copy-start = (f32[8,4,128,128]{3,2,1,0:T(8,128)S(1)}, f32[8,4,128,128]{3,2,1,0:T(8,128)}, u32[]{:S(2)}) copy-start(f32[8,4,128,128]{3,2,1,0:T(8,128)} %param.46) | copy-start | bytes 6291460
  0.6 27.7 %copy-start.1 = (f32[8,3,128]{2,0,1:T(8,128)S(1)}, f32[8,3,128]{2,0,1:T(8,128)}, u32[]{:S(2)}) copy-start(f32[8,3,128]{2,0,1:T(8,128)} %param.50) | copy-start | bytes 36868
  0.7 26.2 %copy-start.20 = (s32[8,4]{0,1:T(4,128)S(1)}, s32[8,4]{0,1:T(4,128)}, u32[]{:S(2)}) copy-start(s32[8,4]{0,1:T(4,128)} %param.47) | copy-start | bytes 388
  0.7 30.9 %copy-start.18 = (f32[128,3,128]{2,0,1:T(8,128)S(1)}, f32[128,3,128]{2,0,1:T(8,128)}, u32[]{:S(2)}) copy-start(f32[128,3,128]{2,0,1:T(8,128)} %param.41) | copy-start | bytes 589828
  1.7 29.9 %copy-start.25 = (f32[8,3,128]{2,0,1:T(8,128)S(1)}, f32[8,3,128]{2,0,1:T(8,128)}, u32[]{:S(2)}) copy-start(f32[8,3,128]{2,0,1:T(8,128)} %param.45) | copy-start | bytes 36868
  3.3 248.8 %copy-start.26 = (s32[128]{0:T(128)}, s32[128]{0:T(128)S(1)}, u32[]{:S(2)}) copy-start(s32[128]{0:T(128)S(1)} %fusion.166) | copy-start | bytes 1540
  6.5 38.7 %all-to-all-start = ((s32[128,2,2]{1,2,0:T(2,128)}), s32[128,2,2]{1,2,0:T(2,128)S(1)}, u32[]{:S(2)}, u32[]{:S(2)}) async-start(s32[128,2,2]{1,2,0:T(2,128)} %copy.261), calls=%async_computation | async-start | bytes 262144 | tf_op jit(solution)/shard_map/all_to_all | solution.py:134
  19.6 43.4 %collective-permute-start.1 = (f32[5,8,1,128]{3,1,2,0:T(8,128)}, f32[5,8,1,128]{3,1,2,0:T(8,128)S(1)}, u32[]{:S(2)}, u32[]{:S(2)}) collective-permute-start(f32[5,8,1,128]{3,1,2,0:T(8,128)} %bitcast.176), channel_id=1, source_target_pairs={{8,0},{16,8},{24,16},{32,24},{40,32},{48,40},{56,48},{64,56},{72,6... | collective-permute-start | bytes 61448 | tf_op jit(solution)/shard_map/ppermute | solution.py:27
  25.0 38.0 %collective-permute-start = (f32[5,8,1,128]{3,1,2,0:T(8,128)}, f32[5,8,1,128]{3,1,2,0:T(8,128)S(1)}, u32[]{:S(2)}, u32[]{:S(2)}) collective-permute-start(f32[5,8,1,128]{3,1,2,0:T(8,128)} %bitcast.175), channel_id=1, source_target_pairs={{0,8},{8,16},{16,24},{24,32},{32,40},{40,48},{48,56},{56,64},{64,7... | collective-permute-start | bytes 61448 | tf_op jit(solution)/shard_map/ppermute | solution.py:25
  27.7 279.1 %collective-permute-start.5 = (f32[8,3,128]{2,0,1:T(8,128)}, f32[8,3,128]{2,0,1:T(8,128)}, u32[]{:S(2)}, u32[]{:S(2)}) collective-permute-start(f32[8,3,128]{2,0,1:T(8,128)} %convolution_bitcast_fusion.22), channel_id=1, source_target_pairs={{1,0},{2,1},{3,2},{4,3},{5,4},{6,5},{7,6},{8,7},{9,8},{10,9},{11,1... | collective-permute-start | bytes 36872 | tf_op jit(solution)/shard_map/ppermute | solution.py:27
  28.3 245.9 %collective-permute-start.4 = (f32[8,3,128]{2,1,0:T(4,128)S(1)}, f32[8,3,128]{2,1,0:T(4,128)S(1)}, u32[]{:S(2)}, u32[]{:S(2)}) collective-permute-start(f32[8,3,128]{2,1,0:T(4,128)S(1)} %copy.275), channel_id=1, source_target_pairs={{0,1},{1,2},{2,3},{3,4},{4,5},{5,6},{6,7},{7,8},{8,9},{9,10},{10,1... | collective-permute-start | bytes 36872 | tf_op jit(solution)/shard_map/ppermute | solution.py:25
  30.7 30.1 %copy-start.9 = (f32[5,1,128,128]{3,2,1,0:T(8,128)}, f32[5,1,128,128]{3,2,1,0:T(8,128)S(1)}, u32[]{:S(2)}) copy-start(f32[5,1,128,128]{3,2,1,0:T(8,128)S(1)} %get-tuple-element.226) | copy-start | bytes 983044
  30.7 206.5 %copy-start.28 = (s32[1024]{0:T(1024)}, s32[1024]{0:T(1024)S(1)}, u32[]{:S(2)}) copy-start(s32[1024]{0:T(1024)S(1)} %pad_clamp_fusion.2) | copy-start | bytes 12292
  45.2 65.6 %all-to-all-start.1 = ((f32[256,3,128]{2,1,0:T(4,128)}), f32[256,3,128]{2,1,0:T(4,128)}, u32[]{:S(2)}, u32[]{:S(2)}) async-start(f32[256,3,128]{2,1,0:T(4,128)} %scatter_fusion), calls=%async_computation.1 | async-start | bytes 1048576 | tf_op jit(solution)/shard_map/all_to_all | solution.py:133
  65.0 4.2 copy-start.5
  73.7 13.5 %collective-permute-start.2 = (f32[5,8,130,1]{2,1,3,0:T(8,128)S(1)}, f32[5,8,130,1]{2,1,3,0:T(8,128)}, u32[]{:S(2)}, u32[]{:S(2)}) collective-permute-start(f32[5,8,130,1]{2,1,3,0:T(8,128)S(1)} %copy.253), channel_id=1, source_target_pairs={{0,1},{1,2},{2,3},{3,4},{4,5},{5,6},{6,7},{7,0},{8,9},{9,10},{10,1... | collective-permute-start | bytes 62408 | tf_op jit(solution)/shard_map/ppermute | solution.py:25
  79.2 2.7 copy-start.6
  79.2 11.2 %collective-permute-start.3 = (f32[5,8,130,1]{2,1,3,0:T(8,128)}, f32[5,8,130,1]{2,1,3,0:T(8,128)}, u32[]{:S(2)}, u32[]{:S(2)}) collective-permute-start(f32[5,8,130,1]{2,1,3,0:T(8,128)} %copy.254), channel_id=1, source_target_pairs={{1,0},{2,1},{3,2},{4,3},{5,4},{6,5},{7,6},{0,7},{9,8},{10,9},{11,1... | collective-permute-start | bytes 62408 | tf_op jit(solution)/shard_map/ppermute | solution.py:27
  213.9 23.2 %all-to-all-start.2 = ((f32[256,3,128]{2,1,0:T(4,128)}), f32[256,3,128]{2,1,0:T(4,128)}, u32[]{:S(2)}, u32[]{:S(2)}) async-start(f32[256,3,128]{2,1,0:T(4,128)} %convolution_bitcast_fusion.3), calls=%async_computation.2 | async-start | bytes 1048576 | tf_op jit(solution)/shard_map/all_to_all | solution.py:140
  224.2 14.8 %copy-start.14 = (f32[128,3,128]{2,0,1:T(8,128)S(1)}, f32[128,3,128]{2,0,1:T(8,128)}, u32[]{:S(2)}) copy-start(f32[128,3,128]{2,0,1:T(8,128)} %param.42) | copy-start | bytes 589828
  224.2 15.1 %copy-start.10 = (f32[5,1,128,128]{3,2,1,0:T(8,128)S(1)}, f32[5,1,128,128]{3,2,1,0:T(8,128)}, u32[]{:S(2)}) copy-start(f32[5,1,128,128]{3,2,1,0:T(8,128)} %copy-done.9) | copy-start | bytes 983044
  245.1 2.2 slice-start
  245.5 2.7 copy-start.7
  245.5 3.0 slice-start.1
  251.0 22.8 %copy-start.16 = (f32[8,8,3,128]{3,1,2,0:T(8,128)S(1)}, f32[8,8,3,128]{3,1,2,0:T(8,128)}, u32[]{:S(2)}) copy-start(f32[8,8,3,128]{3,1,2,0:T(8,128)} %param.51) | copy-start | bytes 294916
  264.5 22.7 %all-to-all-start.3 = ((f32[256,3,128]{2,1,0:T(4,128)}), f32[256,3,128]{2,1,0:T(4,128)S(1)}, u32[]{:S(2)}, u32[]{:S(2)}) async-start(f32[256,3,128]{2,1,0:T(4,128)} %scatter_fusion.1), calls=%async_computation.3 | async-start | bytes 1048576 | tf_op jit(solution)/shard_map/all_to_all | solution.py:140
  274.3 32.6 %copy-start.23 = (s32[256,2]{0,1:T(2,128)}, s32[256,2]{0,1:T(2,128)S(1)}, u32[]{:S(2)}) copy-start(s32[256,2]{0,1:T(2,128)S(1)} %eq.26) | copy-start | bytes 6148
  276.7 30.1 %copy-start.19 = (f32[8,128]{1,0:T(8,128)S(1)}, f32[8,128]{1,0:T(8,128)}, u32[]{:S(2)}) copy-start(f32[8,128]{1,0:T(8,128)} %param.48) | copy-start | bytes 12292
  276.7 30.1 %copy-start.22 = (f32[8,3,128]{2,0,1:T(8,128)S(1)}, f32[8,3,128]{2,0,1:T(8,128)}, u32[]{:S(2)}) copy-start(f32[8,3,128]{2,0,1:T(8,128)} %param.49) | copy-start | bytes 36868
  308.0 2.5 collective-permute-start.6
  310.5 3.1 collective-permute-start.7
  312.9 283.9 %copy-start.17 = (f32[8,8,3,128]{3,1,2,0:T(8,128)S(1)}, f32[8,8,3,128]{3,1,2,0:T(8,128)}, u32[]{:S(2)}) copy-start(f32[8,8,3,128]{3,1,2,0:T(8,128)} %param.52) | copy-start | bytes 294916
  452.1 3.0 collective-permute-start.8
  455.1 3.4 collective-permute-start.9
  630.9 19.1 %all-to-all-start.4 = ((f32[256,3,128]{2,1,0:T(4,128)}), f32[256,3,128]{2,1,0:T(4,128)S(1)}, u32[]{:S(2)}, u32[]{:S(2)}) async-start(f32[256,3,128]{2,1,0:T(4,128)} %convolution_bitcast_fusion.2), calls=%async_computation.4 | async-start | bytes 1048576 | tf_op jit(solution)/shard_map/all_to_all | solution.py:140
  637.1 47.1 %collective-permute-start.10 = (f32[8,3,128]{2,0,1:T(8,128)S(1)}, f32[8,3,128]{2,0,1:T(8,128)S(1)}, u32[]{:S(2)}, u32[]{:S(2)}) collective-permute-start(f32[8,3,128]{2,0,1:T(8,128)S(1)} %bitcast_subtract_fusion.1), channel_id=1, source_target_pairs={{0,1},{1,2},{2,3},{3,4},{4,5},{5,6},{6,7},{7,8},{8,9},{9,10},{10,1... | collective-permute-start | bytes 36872 | tf_op jit(solution)/shard_map/ppermute | solution.py:25
  655.7 1.8 copy-start.11
  660.7 2.6 copy-start.15
  660.7 3.7 copy-start.27
  676.8 18.1 %all-to-all-start.5 = ((f32[256,3,128]{2,1,0:T(4,128)}), f32[256,3,128]{2,1,0:T(4,128)S(1)}, u32[]{:S(2)}, u32[]{:S(2)}) async-start(f32[256,3,128]{2,1,0:T(4,128)} %scatter_fusion.2), calls=%async_computation.5 | async-start | bytes 1048576 | tf_op jit(solution)/shard_map/all_to_all | solution.py:140
  682.8 31.9 %collective-permute-start.11 = (f32[8,3,128]{2,0,1:T(8,128)S(1)}, f32[8,3,128]{2,0,1:T(8,128)S(1)}, u32[]{:S(2)}, u32[]{:S(2)}) collective-permute-start(f32[8,3,128]{2,0,1:T(8,128)S(1)} %convolution_bitcast_fusion.18), channel_id=1, source_target_pairs={{1,0},{2,1},{3,2},{4,3},{5,4},{6,5},{7,6},{8,7},{9,8},{10,9},{11,1... | collective-permute-start | bytes 36872 | tf_op jit(solution)/shard_map/ppermute | solution.py:27
  686.7 28.0 %copy-start.24 = (s32[256,2]{0,1:T(2,128)S(1)}, s32[256,2]{0,1:T(2,128)}, u32[]{:S(2)}) copy-start(s32[256,2]{0,1:T(2,128)} %copy-done.23) | copy-start | bytes 6148
  715.1 2.5 collective-permute-start.12
  717.5 3.1 collective-permute-start.13
  720.0 284.1 %slice-start.2 = ((f32[8,8,3,128]{3,1,2,0:T(8,128)}), f32[7,8,3,128]{3,1,2,0:T(8,128)S(1)}, s32[]{:S(2)}) async-start(f32[8,8,3,128]{3,1,2,0:T(8,128)} %param.52), calls=%async_computation.8 | async-start | bytes 172032 | tf_op jit(solution)/shard_map/slice | solution.py:249
  858.9 3.2 collective-permute-start.14
  862.0 3.4 collective-permute-start.15
  937.8 67.2 %copy-start.21 = (f32[8,3,128]{2,0,1:T(8,128)}, f32[8,3,128]{2,0,1:T(8,128)S(1)}, u32[]{:S(2)}) copy-start(f32[8,3,128]{2,0,1:T(8,128)S(1)} %get-tuple-element.201) | copy-start | bytes 36868
  (6 other events, 9.5 us)
where the time goes:
time: 1010 us
  blocking collectives  535 us (53%)
  matrix products  127 us (13%)
  local copies, waits for them, and re-layouts  113 us (11%)
  other arithmetic  113 us (11%)
  starting transfers between devices  74.2 us (7%)
  waiting for transfers between devices  34.2 us (3%)
    psum x8, blocking collectives, global_sums(): return lax.psum(values, ('fx', 'fy'))  535 us
    dot_general x2, matrix products, owner_motion(): jnp.einsum('gkij,gkcj->gci', kernels, field_values[support], precision=TO...  63.6 us
    dynamic_update_slice x16, other arithmetic, owner_kernels(): lax.map(one_group, (places.reshape(-1, group, 3, points), support.reshape...  43.5 us
    dot_general x2, matrix products, owner_loads(): jnp.einsum('gkij,gci->gkcj', kernels, traction, precision=TOP_PRECISION)  39.3 us
    scatter x4, local copies, waits for them, and re-layouts, pack(): jnp.zeros((width,) + values.shape[1:], values.dtype).at[slots].set(values)  38.3 us
    all_to_all x4, waiting for transfers between devices, route_field(): lax.all_to_all(values, ('fx', 'fy'), split_axis=0, concat_axis=0, tiled=T...  30.9 us
    all_to_all x4, starting transfers between devices, route_field(): lax.all_to_all(values, ('fx', 'fy'), split_axis=0, concat_axis=0, tiled=T...  29.5 us
  transfers between devices with their start and end apart: 22, of which 8 were waited for; matrix products, arithmetic and copies ran while one was open for 29% of the time, Pallas kernels for 0%

commit v1 on v0

--- a/solution.py
+++ b/solution.py
@@ -141,7 +141,7 @@
 
 
 def global_sums(values):
-    return lax.psum(values, ("fx", "fy"))
+    return jnp.sum(lax.all_gather(values, ("fx", "fy")), axis=0)
 
 
 def stiffness(field_values, couplings, sparsity_layout, selector, diagonal):

time: 1010 us -> 967 us (0.957)
  blocking collectives: 535 us -> 478 us
    psum x8 -> x0, blocking collectives: 535 us -> none  [global_sums(): return lax.psum(values, ('fx', 'fy'))]
    unnamed x0 -> x6, blocking collectives: none -> 409 us
    all_gather x0 -> x2, blocking collectives: none -> 68.7 us  [global_sums(): return jnp.sum(lax.all_gather(values, ('fx', 'fy')), axis=0)]
  transfers between devices with their start and end apart: 22 -> 22, of which waited for: 8 -> 8; matrix products, arithmetic and copies ran while one was open for 29% -> 30% of each run, Pallas kernels for 0% -> 0%
where the time goes in v1:
time: 967 us; the launch traced here: 959 us
  blocking collectives  478 us (49%)
  matrix products  127 us (13%)
  local copies, waits for them, and re-layouts  119 us (12%)
  other arithmetic  118 us (12%)
  starting transfers between devices  73.4 us (8%)
  waiting for transfers between devices  34.1 us (4%)
    unnamed x6, blocking collectives  409 us
    all_gather x2, blocking collectives, global_sums(): return jnp.sum(lax.all_gather(values, ('fx', 'fy')), axis=0)  68.7 us
    dot_general x2, matrix products, owner_motion(): jnp.einsum('gkij,gkcj->gci', kernels, field_values[support], precision=TO...  63.6 us
    dynamic_update_slice x16, other arithmetic, owner_kernels(): lax.map(one_group, (places.reshape(-1, group, 3, points), support.reshape...  43.5 us
    dot_general x2, matrix products, owner_loads(): jnp.einsum('gkij,gci->gkcj', kernels, traction, precision=TOP_PRECISION)  39.3 us
    scatter x4, local copies, waits for them, and re-layouts, pack(): jnp.zeros((width,) + values.shape[1:], values.dtype).at[slots].set(values)  38.3 us
    all_to_all x4, waiting for transfers between devices, route_field(): lax.all_to_all(values, ('fx', 'fy'), split_axis=0, concat_axis=0, tiled=T...  30.8 us
    all_to_all x4, starting transfers between devices, route_field(): lax.all_to_all(values, ('fx', 'fy'), split_axis=0, concat_axis=0, tiled=T...  28.9 us
  transfers between devices with their start and end apart: 22, of which 8 were waited for; matrix products, arithmetic and copies ran while one was open for 30% of the time, Pallas kernels for 0%

profile of v1, /device:TPU:1, one launch (start us, length us, event | category | flops | bytes accessed | tf_op | source)
XLA Modules:
  0.0 959.1 jit_solution(6957689528994456781)
XLA Ops:
  6.5 11.5 %all-to-all-start = ((s32[128,2,2]{1,2,0:T(2,128)}), s32[128,2,2]{1,2,0:T(2,128)S(1)}, u32[]{:S(2)}, u32[]{:S(2)}) async-start(s32[128,2,2]{1,2,0:T(2,128)} %copy.346), calls=%async_computation | async-start | bytes 262144 | tf_op jit(solution)/shard_map/all_to_all | solution.py:134
  19.6 5.4 collective-permute-start.1
  32.7 12.5 %scatter_fusion = f32[256,3,128]{2,1,0:T(4,128)} fusion(f32[256,3,128]{2,1,0:T(4,128)} %broadcast.438.clone, s32[128]{0:T(128)S(1)} %fusion.166, f32[128,3,128]{2,1,0:T(4,128)S(1)} %copy.350), kind=kCustom, calls=%fused_computation.12 | custom fusion | bytes 590336 | tf_op jit(solution)/shard_map/scatter | solution.py:214
  45.2 14.9 %all-to-all-start.1 = ((f32[256,3,128]{2,1,0:T(4,128)}), f32[256,3,128]{2,1,0:T(4,128)}, u32[]{:S(2)}, u32[]{:S(2)}) async-start(f32[256,3,128]{2,1,0:T(4,128)} %scatter_fusion), calls=%async_computation.1 | async-start | bytes 1048576 | tf_op jit(solution)/shard_map/all_to_all | solution.py:133
  64.9 3.3 fusion.182
  70.3 3.3 copy.338
  75.2 3.9 copy.339
  87.0 3.2 copy.340
  90.3 3.2 copy.341
  93.5 5.9 pad_maximum_fusion
  100.6 3.1 slice_multiply_fusion
  103.7 3.0 fusion.26
  112.5 69.4 %while.20 = (s32[]{:T(128)}, f32[16,16,2,128,128]{4,3,2,1,0:T(8,128)}, f32[16,16,3,128]{3,1,2,0:T(8,128)}, s32[16,16,2]{1,0,2:T(8,128)S(1)}, f32[8,3,128]{2,1,0:T(4,128)S(1)}, /*index=5*/s32[]{:T(128)}) while((s32[]{:T(128)}, f32[16,16,2,128,128]{4,3,2,1,0:T(8,128)}, f32[16,16,3,128]{3,1,2,0:T(8,128)}, s32[16,16,2]{1,0,2:T(8,128)S(1)}, ...), condition=%wide.region_5.6_spmd, body=%wide.region_4.5_spmd.sunk | while | flops 8389730 | bytes 2471257 | solution.py:113
  114.1 2.8 fusion.215
  118.5 2.7 fusion.215
  122.8 2.7 fusion.215
  127.2 2.7 fusion.215
  131.5 2.7 fusion.215
  140.2 2.7 fusion.215
  144.5 2.7 fusion.215
  148.8 2.8 fusion.215
  153.2 2.7 fusion.215
  157.5 2.7 fusion.215
  161.9 2.7 fusion.215
  166.2 2.7 fusion.215
  179.2 2.7 fusion.215
  181.9 32.0 %convolution_bitcast_fusion.3 = f32[256,3,128]{2,1,0:T(4,128)} fusion(f32[256,2,128,128]{3,2,1,0:T(8,128)} %bitcast.475, f32[256,2,3,128]{3,1,0,2:T(2,128)S(1)} %bitcast.481), kind=kOutput, calls=%fused_computation.76 | convolution fusion | flops 301989888 | bytes 34734080 | tf_op jit(solution)/shard_map/gkij,gkcj->gci/dot_general | solution.py:120
  213.9 10.2 %all-to-all-start.2 = ((f32[256,3,128]{2,1,0:T(4,128)}), f32[256,3,128]{2,1,0:T(4,128)}, u32[]{:S(2)}, u32[]{:S(2)}) async-start(f32[256,3,128]{2,1,0:T(4,128)} %convolution_bitcast_fusion.3), calls=%async_computation.2 | async-start | bytes 1048576 | tf_op jit(solution)/shard_map/all_to_all | solution.py:140
  224.2 11.7 %fusion.4 = f32[5,8,128,129]{3,2,1,0:T(8,128)} fusion(f32[5,8,130,1]{3,2,1,0:T(8,128)} %copy.340, f32[5,8,1,128]{3,2,1,0:T(1,128)S(1)} %bitcast.492, f32[5,8,128,128]{3,2,1,0:T(8,128)} %param.40, f32[5,8,1,128]{3,2,1,0:T(1,128)S(1)} %bitcast.497, f32[5,8,130,1]{3,2,1,0:T(8,128)} %copy.341, f32[5,8,128,130]{3,2,1,0:T(8,128)} %fusion.25, f32[8,128,129]{2,1,0:T(8,128)} %fusion.24), kind=kLoop, calls=%fused_computation.29 | loop fusion | flops 7265280 | bytes 11158144 | tf_op jit(solution)/shard_map/sub | solution.py:53
  252.0 12.5 %scatter_fusion.1 = f32[256,3,128]{2,1,0:T(4,128)} fusion(f32[256,3,128]{2,1,0:T(4,128)} %broadcast.438.clone.1, s32[128]{0:T(128)S(1)} %fusion.166, f32[128,3,128]{2,1,0:T(4,128)S(1)} %copy.358), kind=kCustom, calls=%fused_computation.13 | custom fusion | bytes 590336 | tf_op jit(solution)/shard_map/scatter | solution.py:214
  264.5 9.2 all-to-all-start.3
  276.6 10.5 %all-to-all-done.3 = f32[256,3,128]{2,1,0:T(4,128)S(1)} async-done(((f32[256,3,128]{2,1,0:T(4,128)}), f32[256,3,128]{2,1,0:T(4,128)S(1)}, u32[]{:S(2)}, u32[]{:S(2)}) %all-to-all-start.3) | async-done | bytes 393248 | tf_op jit(solution)/shard_map/all_to_all | solution.py:140
  287.1 19.6 %convolution_bitcast_fusion.1 = f32[256,2,3,128]{3,2,1,0:T(4,128)S(1)} fusion(f32[256,2,128,128]{3,2,1,0:T(8,128)} %bitcast.476, f32[256,3,128]{2,1,0:T(4,128)S(1)} %all-to-all-done.3), kind=kOutput, calls=%fused_computation.74 | convolution fusion | flops 301989888 | bytes 34734080 | tf_op jit(solution)/shard_map/gkij,gci->gkcj/dot_general | solution.py:124
  315.6 71.6 %all-reduce.9 = (f32[128]{0:T(128)S(1)}, f32[128]{0:T(128)S(1)}) all-reduce(f32[128]{0:T(128)S(1)} %dynamic-update-slice.34, f32[128]{0:T(128)S(1)} %dynamic-update-slice.35), channel_id=1, replica_groups=mesh['fx'=16,'fy'=8] {'fx','fy'}, use_global_device_ids=true, to_apply=%add | all-reduce | flops 256 | bytes 2048
  391.1 62.7 %all-reduce.2 = f32[128]{0:T(128)S(1)} all-reduce(f32[128]{0:T(128)S(1)} %dynamic-update-slice.36), channel_id=1, replica_groups=mesh['fx'=16,'fy'=8] {'fx','fy'}, use_global_device_ids=true, to_apply=%add.2 | all-reduce | flops 128 | bytes 1024
  463.5 70.3 %all-reduce.3 = f32[128]{0:T(128)S(1)} all-reduce(f32[128]{0:T(128)S(1)} %dynamic-update-slice.37), channel_id=1, replica_groups=mesh['fx'=16,'fy'=8] {'fx','fy'}, use_global_device_ids=true, to_apply=%add.3 | all-reduce | flops 128 | bytes 1024
  536.1 34.4 %all-gather = f32[1024,9]{1,0:T(8,128)S(1)} all-gather(f32[8,9]{1,0:T(8,128)S(1)} %pad_maximum_fusion.17), channel_id=2, replica_groups=mesh['fx'=16,'fy'=8] {'fx','fy'}, dimensions={0}, use_global_device_ids=true | all-gather | bytes 37152 | tf_op jit(solution)/shard_map/all_gather | solution.py:144
  576.4 31.6 %convolution_bitcast_fusion.2 = f32[256,3,128]{2,1,0:T(4,128)} fusion(f32[256,2,3,128]{3,2,1,0:T(4,128)S(1)} %bitcast.482, f32[256,2,128,128]{3,2,1,0:T(8,128)} %bitcast.477), kind=kOutput, calls=%fused_computation.75 | convolution fusion | flops 301989888 | bytes 34734080 | tf_op jit(solution)/shard_map/gkij,gkcj->gci/dot_general | solution.py:120
  608.0 5.0 all-to-all-start.4
  615.9 10.9 %all-to-all-done.4 = f32[256,3,128]{2,1,0:T(4,128)S(1)} async-done(((f32[256,3,128]{2,1,0:T(4,128)}), f32[256,3,128]{2,1,0:T(4,128)S(1)}, u32[]{:S(2)}, u32[]{:S(2)}) %all-to-all-start.4) | async-done | bytes 393248 | tf_op jit(solution)/shard_map/all_to_all | solution.py:140
  641.2 12.5 %scatter_fusion.2 = f32[256,3,128]{2,1,0:T(4,128)} fusion(f32[256,3,128]{2,1,0:T(4,128)} %broadcast.438, s32[128]{0:T(128)S(1)} %copy-done.27, f32[128,3,128]{2,1,0:T(4,128)S(1)} %copy.382), kind=kCustom, calls=%fused_computation.14 | custom fusion | bytes 590336 | tf_op jit(solution)/shard_map/scatter | solution.py:214
  653.6 4.5 all-to-all-start.5
  663.4 8.2 all-to-all-done.5
  671.6 19.6 %convolution_bitcast_fusion = f32[256,2,3,128]{3,2,1,0:T(4,128)S(1)} fusion(f32[256,2,128,128]{3,2,1,0:T(8,128)} %bitcast.478, f32[256,3,128]{2,1,0:T(4,128)S(1)} %all-to-all-done.5), kind=kOutput, calls=%fused_computation.73 | convolution fusion | flops 301989888 | bytes 34734080 | tf_op jit(solution)/shard_map/gkij,gci->gkcj/dot_general | solution.py:124
  699.5 71.6 %all-reduce.8 = (f32[128]{0:T(128)S(1)}, f32[128]{0:T(128)S(1)}) all-reduce(f32[128]{0:T(128)S(1)} %dynamic-update-slice.38, f32[128]{0:T(128)S(1)} %dynamic-update-slice.39), channel_id=1, replica_groups=mesh['fx'=16,'fy'=8] {'fx','fy'}, use_global_device_ids=true, to_apply=%add.4 | all-reduce | flops 256 | bytes 2048
  775.0 62.7 %all-reduce.6 = f32[128]{0:T(128)S(1)} all-reduce(f32[128]{0:T(128)S(1)} %dynamic-update-slice.40), channel_id=1, replica_groups=mesh['fx'=16,'fy'=8] {'fx','fy'}, use_global_device_ids=true, to_apply=%add.6 | all-reduce | flops 128 | bytes 1024
  847.4 70.3 %all-reduce.7 = f32[128]{0:T(128)S(1)} all-reduce(f32[128]{0:T(128)S(1)} %dynamic-update-slice.41), channel_id=1, replica_groups=mesh['fx'=16,'fy'=8] {'fx','fy'}, use_global_device_ids=true, to_apply=%add.7 | all-reduce | flops 128 | bytes 1024
  920.4 34.4 %all-gather.1 = f32[1024,9]{1,0:T(8,128)S(1)} all-gather(f32[8,9]{1,0:T(8,128)S(1)} %pad_maximum_fusion.18), channel_id=3, replica_groups=mesh['fx'=16,'fy'=8] {'fx','fy'}, dimensions={0}, use_global_device_ids=true | all-gather | bytes 37152 | tf_op jit(solution)/shard_map/all_gather | solution.py:144
  (424 shorter events, 164.6 us)
Async XLA Ops:
  0.6 24.4 %copy-start = (f32[8,4,128,128]{3,2,1,0:T(8,128)S(1)}, f32[8,4,128,128]{3,2,1,0:T(8,128)}, u32[]{:S(2)}) copy-start(f32[8,4,128,128]{3,2,1,0:T(8,128)} %param.46) | copy-start | bytes 6291460
  0.6 27.7 %copy-start.1 = (f32[8,3,128]{2,0,1:T(8,128)S(1)}, f32[8,3,128]{2,0,1:T(8,128)}, u32[]{:S(2)}) copy-start(f32[8,3,128]{2,0,1:T(8,128)} %param.50) | copy-start | bytes 36868
  0.7 26.2 %copy-start.20 = (s32[8,4]{0,1:T(4,128)S(1)}, s32[8,4]{0,1:T(4,128)}, u32[]{:S(2)}) copy-start(s32[8,4]{0,1:T(4,128)} %param.47) | copy-start | bytes 388
  0.7 30.8 %copy-start.18 = (f32[128,3,128]{2,0,1:T(8,128)S(1)}, f32[128,3,128]{2,0,1:T(8,128)}, u32[]{:S(2)}) copy-start(f32[128,3,128]{2,0,1:T(8,128)} %param.41) | copy-start | bytes 589828
  1.7 29.9 %copy-start.25 = (f32[8,3,128]{2,0,1:T(8,128)S(1)}, f32[8,3,128]{2,0,1:T(8,128)}, u32[]{:S(2)}) copy-start(f32[8,3,128]{2,0,1:T(8,128)} %param.45) | copy-start | bytes 36868
  3.3 248.8 %copy-start.26 = (s32[128]{0:T(128)}, s32[128]{0:T(128)S(1)}, u32[]{:S(2)}) copy-start(s32[128]{0:T(128)S(1)} %fusion.166) | copy-start | bytes 1540
  6.5 38.7 %all-to-all-start = ((s32[128,2,2]{1,2,0:T(2,128)}), s32[128,2,2]{1,2,0:T(2,128)S(1)}, u32[]{:S(2)}, u32[]{:S(2)}) async-start(s32[128,2,2]{1,2,0:T(2,128)} %copy.346), calls=%async_computation | async-start | bytes 262144 | tf_op jit(solution)/shard_map/all_to_all | solution.py:134
  19.6 43.3 %collective-permute-start.1 = (f32[5,8,1,128]{3,1,2,0:T(8,128)}, f32[5,8,1,128]{3,1,2,0:T(8,128)S(1)}, u32[]{:S(2)}, u32[]{:S(2)}) collective-permute-start(f32[5,8,1,128]{3,1,2,0:T(8,128)} %bitcast.174), channel_id=1, source_target_pairs={{8,0},{16,8},{24,16},{32,24},{40,32},{48,40},{56,48},{64,56},{72,6... | collective-permute-start | bytes 61448 | tf_op jit(solution)/shard_map/ppermute | solution.py:27
  25.0 37.9 %collective-permute-start = (f32[5,8,1,128]{3,1,2,0:T(8,128)}, f32[5,8,1,128]{3,1,2,0:T(8,128)S(1)}, u32[]{:S(2)}, u32[]{:S(2)}) collective-permute-start(f32[5,8,1,128]{3,1,2,0:T(8,128)} %bitcast.173), channel_id=1, source_target_pairs={{0,8},{8,16},{16,24},{24,32},{32,40},{40,48},{48,56},{56,64},{64,7... | collective-permute-start | bytes 61448 | tf_op jit(solution)/shard_map/ppermute | solution.py:25
  27.7 279.0 %collective-permute-start.5 = (f32[8,3,128]{2,0,1:T(8,128)}, f32[8,3,128]{2,0,1:T(8,128)}, u32[]{:S(2)}, u32[]{:S(2)}) collective-permute-start(f32[8,3,128]{2,0,1:T(8,128)} %convolution_bitcast_fusion.22), channel_id=1, source_target_pairs={{1,0},{2,1},{3,2},{4,3},{5,4},{6,5},{7,6},{8,7},{9,8},{10,9},{11,1... | collective-permute-start | bytes 36872 | tf_op jit(solution)/shard_map/ppermute | solution.py:27
  28.3 245.8 %collective-permute-start.4 = (f32[8,3,128]{2,1,0:T(4,128)S(1)}, f32[8,3,128]{2,1,0:T(4,128)S(1)}, u32[]{:S(2)}, u32[]{:S(2)}) collective-permute-start(f32[8,3,128]{2,1,0:T(4,128)S(1)} %copy.360), channel_id=1, source_target_pairs={{0,1},{1,2},{2,3},{3,4},{4,5},{5,6},{6,7},{7,8},{8,9},{9,10},{10,1... | collective-permute-start | bytes 36872 | tf_op jit(solution)/shard_map/ppermute | solution.py:25
  30.7 29.9 %copy-start.9 = (f32[5,1,128,128]{3,2,1,0:T(8,128)}, f32[5,1,128,128]{3,2,1,0:T(8,128)S(1)}, u32[]{:S(2)}) copy-start(f32[5,1,128,128]{3,2,1,0:T(8,128)S(1)} %get-tuple-element.234) | copy-start | bytes 983044
  30.7 206.4 %copy-start.28 = (s32[1024]{0:T(1024)}, s32[1024]{0:T(1024)S(1)}, u32[]{:S(2)}) copy-start(s32[1024]{0:T(1024)S(1)} %pad_clamp_fusion.2) | copy-start | bytes 12292
  45.2 65.5 %all-to-all-start.1 = ((f32[256,3,128]{2,1,0:T(4,128)}), f32[256,3,128]{2,1,0:T(4,128)}, u32[]{:S(2)}, u32[]{:S(2)}) async-start(f32[256,3,128]{2,1,0:T(4,128)} %scatter_fusion), calls=%async_computation.1 | async-start | bytes 1048576 | tf_op jit(solution)/shard_map/all_to_all | solution.py:133
  64.9 4.2 copy-start.5
  73.6 13.5 %collective-permute-start.2 = (f32[5,8,130,1]{2,1,3,0:T(8,128)S(1)}, f32[5,8,130,1]{2,1,3,0:T(8,128)}, u32[]{:S(2)}, u32[]{:S(2)}) collective-permute-start(f32[5,8,130,1]{2,1,3,0:T(8,128)S(1)} %copy.338), channel_id=1, source_target_pairs={{0,1},{1,2},{2,3},{3,4},{4,5},{5,6},{6,7},{7,0},{8,9},{9,10},{10,1... | collective-permute-start | bytes 62408 | tf_op jit(solution)/shard_map/ppermute | solution.py:25
  79.1 2.7 copy-start.6
  79.1 11.2 %collective-permute-start.3 = (f32[5,8,130,1]{2,1,3,0:T(8,128)}, f32[5,8,130,1]{2,1,3,0:T(8,128)}, u32[]{:S(2)}, u32[]{:S(2)}) collective-permute-start(f32[5,8,130,1]{2,1,3,0:T(8,128)} %copy.339), channel_id=1, source_target_pairs={{1,0},{2,1},{3,2},{4,3},{5,4},{6,5},{7,6},{0,7},{9,8},{10,9},{11,1... | collective-permute-start | bytes 62408 | tf_op jit(solution)/shard_map/ppermute | solution.py:27
  213.9 23.2 %all-to-all-start.2 = ((f32[256,3,128]{2,1,0:T(4,128)}), f32[256,3,128]{2,1,0:T(4,128)}, u32[]{:S(2)}, u32[]{:S(2)}) async-start(f32[256,3,128]{2,1,0:T(4,128)} %convolution_bitcast_fusion.3), calls=%async_computation.2 | async-start | bytes 1048576 | tf_op jit(solution)/shard_map/all_to_all | solution.py:140
  224.1 14.8 %copy-start.14 = (f32[128,3,128]{2,0,1:T(8,128)S(1)}, f32[128,3,128]{2,0,1:T(8,128)}, u32[]{:S(2)}) copy-start(f32[128,3,128]{2,0,1:T(8,128)} %param.42) | copy-start | bytes 589828
  224.1 15.1 %copy-start.10 = (f32[5,1,128,128]{3,2,1,0:T(8,128)S(1)}, f32[5,1,128,128]{3,2,1,0:T(8,128)}, u32[]{:S(2)}) copy-start(f32[5,1,128,128]{3,2,1,0:T(8,128)} %copy-done.9) | copy-start | bytes 983044
  245.0 2.2 slice-start
  245.5 2.7 copy-start.7
  245.5 3.0 slice-start.1
  250.9 22.7 %copy-start.16 = (f32[8,8,3,128]{3,1,2,0:T(8,128)S(1)}, f32[8,8,3,128]{3,1,2,0:T(8,128)}, u32[]{:S(2)}) copy-start(f32[8,8,3,128]{3,1,2,0:T(8,128)} %param.51) | copy-start | bytes 294916
  264.5 22.6 %all-to-all-start.3 = ((f32[256,3,128]{2,1,0:T(4,128)}), f32[256,3,128]{2,1,0:T(4,128)S(1)}, u32[]{:S(2)}, u32[]{:S(2)}) async-start(f32[256,3,128]{2,1,0:T(4,128)} %scatter_fusion.1), calls=%async_computation.3 | async-start | bytes 1048576 | tf_op jit(solution)/shard_map/all_to_all | solution.py:140
  274.1 32.6 %copy-start.23 = (s32[256,2]{0,1:T(2,128)}, s32[256,2]{0,1:T(2,128)S(1)}, u32[]{:S(2)}) copy-start(s32[256,2]{0,1:T(2,128)S(1)} %eq.26) | copy-start | bytes 6148
  276.6 30.1 %copy-start.19 = (f32[8,128]{1,0:T(8,128)S(1)}, f32[8,128]{1,0:T(8,128)}, u32[]{:S(2)}) copy-start(f32[8,128]{1,0:T(8,128)} %param.48) | copy-start | bytes 12292
  276.6 30.1 %copy-start.22 = (f32[8,3,128]{2,0,1:T(8,128)S(1)}, f32[8,3,128]{2,0,1:T(8,128)}, u32[]{:S(2)}) copy-start(f32[8,3,128]{2,0,1:T(8,128)} %param.49) | copy-start | bytes 36868
  307.9 2.5 collective-permute-start.6
  310.3 3.1 collective-permute-start.7
  455.7 3.0 collective-permute-start.8
  457.4 116.4 %copy-start.17 = (f32[8,8,3,128]{3,1,2,0:T(8,128)S(1)}, f32[8,8,3,128]{3,1,2,0:T(8,128)}, u32[]{:S(2)}) copy-start(f32[8,8,3,128]{3,1,2,0:T(8,128)} %param.52) | copy-start | bytes 294916
  458.7 3.4 collective-permute-start.9
  608.0 18.8 %all-to-all-start.4 = ((f32[256,3,128]{2,1,0:T(4,128)}), f32[256,3,128]{2,1,0:T(4,128)S(1)}, u32[]{:S(2)}, u32[]{:S(2)}) async-start(f32[256,3,128]{2,1,0:T(4,128)} %convolution_bitcast_fusion.2), calls=%async_computation.4 | async-start | bytes 1048576 | tf_op jit(solution)/shard_map/all_to_all | solution.py:140
  614.0 47.0 %collective-permute-start.10 = (f32[8,3,128]{2,0,1:T(8,128)S(1)}, f32[8,3,128]{2,0,1:T(8,128)S(1)}, u32[]{:S(2)}, u32[]{:S(2)}) collective-permute-start(f32[8,3,128]{2,0,1:T(8,128)S(1)} %bitcast_subtract_fusion.1), channel_id=1, source_target_pairs={{0,1},{1,2},{2,3},{3,4},{4,5},{5,6},{6,7},{7,8},{8,9},{9,10},{10,1... | collective-permute-start | bytes 36872 | tf_op jit(solution)/shard_map/ppermute | solution.py:25
  632.5 1.8 copy-start.11
  637.5 2.6 copy-start.15
  637.5 3.7 copy-start.27
  653.6 18.0 %all-to-all-start.5 = ((f32[256,3,128]{2,1,0:T(4,128)}), f32[256,3,128]{2,1,0:T(4,128)S(1)}, u32[]{:S(2)}, u32[]{:S(2)}) async-start(f32[256,3,128]{2,1,0:T(4,128)} %scatter_fusion.2), calls=%async_computation.5 | async-start | bytes 1048576 | tf_op jit(solution)/shard_map/all_to_all | solution.py:140
  659.4 31.9 %collective-permute-start.11 = (f32[8,3,128]{2,0,1:T(8,128)S(1)}, f32[8,3,128]{2,0,1:T(8,128)S(1)}, u32[]{:S(2)}, u32[]{:S(2)}) collective-permute-start(f32[8,3,128]{2,0,1:T(8,128)S(1)} %convolution_bitcast_fusion.18), channel_id=1, source_target_pairs={{1,0},{2,1},{3,2},{4,3},{5,4},{6,5},{7,6},{8,7},{9,8},{10,9},{11,1... | collective-permute-start | bytes 36872 | tf_op jit(solution)/shard_map/ppermute | solution.py:27
  663.4 27.9 %copy-start.24 = (s32[256,2]{0,1:T(2,128)S(1)}, s32[256,2]{0,1:T(2,128)}, u32[]{:S(2)}) copy-start(s32[256,2]{0,1:T(2,128)} %copy-done.23) | copy-start | bytes 6148
  691.7 2.5 collective-permute-start.12
  694.2 3.1 collective-permute-start.13
  839.6 3.0 collective-permute-start.14
  841.3 116.8 %slice-start.2 = ((f32[8,8,3,128]{3,1,2,0:T(8,128)}), f32[7,8,3,128]{3,1,2,0:T(8,128)S(1)}, s32[]{:S(2)}) async-start(f32[8,8,3,128]{3,1,2,0:T(8,128)} %param.52), calls=%async_computation.8 | async-start | bytes 172032 | tf_op jit(solution)/shard_map/slice | solution.py:249
  842.6 3.4 collective-permute-start.15
  919.7 39.3 %copy-start.21 = (f32[8,3,128]{2,0,1:T(8,128)}, f32[8,3,128]{2,0,1:T(8,128)S(1)}, u32[]{:S(2)}) copy-start(f32[8,3,128]{2,0,1:T(8,128)S(1)} %get-tuple-element.209) | copy-start | bytes 36868
  (6 other events, 9.5 us)
